TPU v7x, 128 devices: a whole 4x4x4 slice. The times are simulated.
128 devices in a mesh: slab: 32 (over y, z, core), col: 4 (over x).
Axes of the slice: x: 4, y: 4, z: 4, core: 2. Of those that a mesh axis runs over, the one named last changes fastest.
Arguments:
- input_map: float32 [64, 64, 192, 128], P('col', 'slab'), may hold values from -24 to 24
- output_map: float32 [64, 64, 192, 128], P('col', 'slab'), may hold values from -24 to 24
- region_ids: int32 [64, 192, 128], P('slab'), may hold values from 0 to 7
- region_cond: float32 [8], replicated, may hold values from 0.3 to 3
- shift_ids: int32 [2], replicated, may hold values from 0 to 7
Outputs:
- ctrl_factor: float32 [2, 64, 64, 192, 128], P(None, None, 'slab', 'col')
- obsv_factor: float32 [2, 64, 64, 192, 128], P(None, None, 'slab', 'col')
- cross_gram: float32 [128, 128], P('slab', 'col')
All inputs are finite; a program needn't handle non-finite values.
Results may differ from a plain program's by a relative error of at most 0.000098.
Values sent between devices are 32-bit elements; how exact they have to be, the bound alone decides.
A program may use at most 192 MiB of HBM per device.

v0:
```python
import math
import jax
import jax.numpy as jnp
from jax import lax
from jax.sharding import PartitionSpec as P

ADI = 2
STEPS = 3


def extended(block, sides, width):
    for axis, dim in sides:
        count = lax.axis_size(axis)
        forward = [(i, i + 1) for i in range(count - 1)]
        backward = [(target, source) for source, target in forward]
        low = lax.ppermute(
            lax.slice_in_dim(block, block.shape[dim] - width, None, axis=dim), axis, forward
        )
        high = lax.ppermute(lax.slice_in_dim(block, 0, width, axis=dim), axis, backward)
        block = jnp.concatenate([low, block, high], axis=dim)
    return block


def lookup(region_ids, region_cond):
    summed = jnp.zeros(region_ids.shape, jnp.float32)
    for region in range(region_cond.shape[0]):
        summed = summed + jnp.where(region_ids == region, region_cond[region], jnp.float32(0.0))
    return summed


def conduction(field_in, cond_ext):
    centre = field_in[:, 1:-1]
    cond_mid = cond_ext[1:-1]
    summed = 0.5 * (cond_mid + cond_ext[2:]) * (centre - field_in[:, 2:])
    summed = summed + 0.5 * (cond_mid + cond_ext[:-2]) * (centre - field_in[:, :-2])
    cond_y = jnp.pad(cond_mid, ((0, 0), (1, 1), (0, 0)))
    field_y = jnp.pad(centre, ((0, 0), (0, 0), (1, 1), (0, 0)))
    summed = summed + 0.5 * (cond_mid + cond_y[:, 2:]) * (centre - field_y[:, :, 2:])
    summed = summed + 0.5 * (cond_mid + cond_y[:, :-2]) * (centre - field_y[:, :, :-2])
    cond_z = jnp.pad(cond_mid, ((0, 0), (0, 0), (1, 1)))
    field_z = jnp.pad(centre, ((0, 0), (0, 0), (0, 0), (1, 1)))
    summed = summed + 0.5 * (cond_mid + cond_z[:, :, 2:]) * (centre - field_z[:, :, :, 2:])
    summed = summed + 0.5 * (cond_mid + cond_z[:, :, :-2]) * (centre - field_z[:, :, :, :-2])
    return summed


def bounds(shift_val, cond_max):
    high_eig = shift_val + 12.0 * cond_max
    mid_eig = 0.5 * (high_eig + shift_val)
    half_span = 0.5 * (high_eig - shift_val)
    return (mid_eig, half_span, mid_eig / half_span)


def solve_slabs(right_side, shift_val, cond_max, cond_ext):
    mid_eig, half_span, ratio_eig = bounds(shift_val, cond_max)
    rho_now = 1.0 / ratio_eig
    solution = jnp.zeros_like(right_side)
    residual = right_side
    direction = right_side / mid_eig
    for sweep_idx in range(STEPS - 1):
        solution = solution + direction
        padded = extended(direction, (("slab", 1),), 1)
        applied = conduction(padded, cond_ext) + shift_val * direction
        residual = residual - applied
        rho_next = 1.0 / (2.0 * ratio_eig - rho_now)
        direction = rho_next * rho_now * direction + 2.0 * rho_next / half_span * residual
        rho_now = rho_next
    return solution + direction


def run_segments(stacked, shifts, solver):
    factors = []
    current = stacked
    for segment_idx in range(ADI):
        shift_val = shifts[segment_idx]
        if segment_idx == 0:
            current = solver(stacked, shift_val)
        else:
            current = current - (shifts[segment_idx - 1] + shift_val) * solver(current, shift_val)
        factors.append(jnp.sqrt(2.0 * shift_val) * current)
    return jnp.stack(factors)


def body(input_map, output_map, region_ids, region_cond, shift_ids):
    col_local = input_map.shape[0]
    local_x = input_map.shape[1]
    cond_cells = lookup(region_ids, region_cond)
    cond_max = jnp.max(region_cond)
    shifts = 0.25 * jnp.exp2(shift_ids.astype(jnp.float32))
    total_x = local_x * lax.axis_size("slab")
    stacked = jnp.concatenate([input_map, output_map], 0)
    cond_ext = extended(cond_cells, (("slab", 0),), 1)
    factor_stack = run_segments(
        stacked, shifts, lambda rhs, shift_val: solve_slabs(rhs, shift_val, cond_max, cond_ext)
    )
    ctrl_local = factor_stack[:, :col_local]
    obsv_local = factor_stack[:, col_local:]
    ctrl_cols, obsv_cols = (
        lax.all_to_all(ctrl_local, "col", split_axis=3, concat_axis=1, tiled=True),
        lax.all_to_all(obsv_local, "col", split_axis=3, concat_axis=1, tiled=True),
    )
    row_count = ctrl_cols.shape[0] * ctrl_cols.shape[1]
    ctrl_flat = ctrl_cols.reshape(row_count, -1)
    obsv_flat = obsv_cols.reshape(row_count, -1)
    partial_value = lax.dot_general(
        ctrl_flat,
        obsv_flat,
        (((1,), (1,)), ((), ())),
        precision=lax.Precision.HIGHEST,
        preferred_element_type=jnp.float32,
    )
    cells_total = total_x * region_ids.shape[1] * region_ids.shape[2]
    norm_scale = 1.0 / math.sqrt(cells_total)
    whole_sum = lax.psum(partial_value, ("slab", "col"))
    tile_rows = row_count // lax.axis_size("slab")
    tile_cols = row_count // lax.axis_size("col")
    own_tile = lax.dynamic_slice(
        whole_sum,
        (lax.axis_index("slab") * tile_rows, lax.axis_index("col") * tile_cols),
        (tile_rows, tile_cols),
    )
    return (ctrl_cols, obsv_cols, own_tile * norm_scale)


def solution(mesh):
    placed = (
        P("col", "slab", None, None),
        P("col", "slab", None, None),
        P("slab", None, None),
        P(),
        P(),
    )
    return jax.shard_map(
        body,
        mesh=mesh,
        in_specs=placed,
        out_specs=(
            P(None, None, "slab", "col", None),
            P(None, None, "slab", "col", None),
            P("slab", "col"),
        ),
        check_vma=False,
    )
```

profile of v0, /device:TPU:1, one launch (start us, length us, event | category | flops | bytes accessed | tf_op | source)
XLA Modules:
  0.0 643.6 jit_solution(5252572299411760887)
XLA Ops:
  11.8 3.9 constant_dynamic-update-slice_fusion.1
  17.6 3.2 broadcast_divide_fusion.1
  20.9 3.3 fusion.105
  25.4 3.3 collective-permute-start.1
  28.8 3.5 collective-permute-start.3
  33.0 5.2 select_add_fusion
  44.6 22.0 %collective-permute-done = f32[1,192,128]{2,1,0:T(8,128)S(1)} collective-permute-done((f32[1,192,128]{2,1,0:T(8,128)S(1)}, f32[1,192,128]{2,1,0:T(8,128)S(1)}, u32[]{:S(2)}, u32[]{:S(2)}) %collective-permute-start) | collective-permute-done | bytes 98336 | tf_op jit(solution)/shard_map/ppermute | solution.py:19
  68.0 23.3 %multiply_add_fusion.1 = (f32[32,2,192,128]{3,2,1,0:T(8,128)S(1)}, f32[32,2,192,128]{3,2,1,0:T(8,128)}) fusion(f32[32,2,192,128]{3,2,1,0:T(8,128)} %copy-done.1, f32[]{:T(128)S(6)} %div.53, f32[]{:T(128)S(6)} %mul.354, f32[32,2,192,128]{3,2,1,0:T(8,128)} %constant_dynamic-update-slice_fusion, f32[]{:T(128)} %bitcast, ...), kind=kLoop, calls=%fused_computation.116 | loop fusion | flops 39321600 | bytes 32636940 | tf_op jit(solution)/shard_map/add | solution.py:66
  91.3 3.2 fusion.104
  97.8 4.4 collective-permute-start.5
  103.6 32.0 %collective-permute-done.4 = f32[32,1,192,128]{3,2,1,0:T(8,128)} collective-permute-done((f32[32,1,192,128]{3,2,1,0:T(8,128)}, f32[32,1,192,128]{3,2,1,0:T(8,128)}, u32[]{:S(2)}, u32[]{:S(2)}) %collective-permute-start.4) | collective-permute-done | bytes 3145760 | tf_op jit(solution)/shard_map/ppermute | solution.py:19
  136.7 26.0 %broadcast_divide_fusion = (f32[32,2,192,128]{3,2,1,0:T(8,128)S(1)}, f32[32,2,192,128]{3,2,1,0:T(8,128)}) fusion(f32[]{:T(128)S(6)} %mul.397, f32[32,2,192,128]{3,2,1,0:T(8,128)} %get-tuple-element.8, f32[32,2,192,128]{3,2,1,0:T(8,128)} %copy-done.3, f32[]{:T(128)} %bitcast, f32[2,192,128]{2,1,0:T(8,128)S(1)} %get-tuple-element.29, ...), kind=kLoop, calls=%fused_computation.117 | loop fusion | flops 45613056 | bytes 38928404 | tf_op jit(solution)/shard_map/div | solution.py:59
  162.7 3.8 fusion.103
  169.2 4.4 collective-permute-start.7
  175.1 31.8 %collective-permute-done.6 = f32[32,1,192,128]{3,2,1,0:T(8,128)} collective-permute-done((f32[32,1,192,128]{3,2,1,0:T(8,128)}, f32[32,1,192,128]{3,2,1,0:T(8,128)}, u32[]{:S(2)}, u32[]{:S(2)}) %collective-permute-start.6) | collective-permute-done | bytes 3145760 | tf_op jit(solution)/shard_map/ppermute | solution.py:19
  208.1 26.6 %multiply_add_fusion = (f32[32,2,192,128]{3,2,1,0:T(8,128)S(1)}, f32[32,2,192,128]{3,2,1,0:T(8,128)}, f32[1,32,2,192,128]{4,3,2,1,0:T(8,128)}) fusion(f32[]{:T(128)S(6)} %div.61, f32[]{:T(128)S(6)} %mul.400, f32[32,2,192,128]{3,2,1,0:T(8,128)} %get-tuple-element.6, f32[]{:T(128)S(6)} %mul.397, f32[32,2,192,128]{3,2,1,0:T(8,128)} %copy-done.2, f32[]{:T(128)} %bitcast.10, ...), kind=kLoop, calls=%fused_computation.114 | loop fusion | flops 42467328 | bytes 38928404 | tf_op jit(solution)/shard_map/add | solution.py:66
  234.7 3.8 fusion.102
  241.2 4.6 collective-permute-start.9
  247.8 31.1 %collective-permute-done.8 = f32[32,1,192,128]{3,2,1,0:T(8,128)} collective-permute-done((f32[32,1,192,128]{3,2,1,0:T(8,128)}, f32[32,1,192,128]{3,2,1,0:T(8,128)}, u32[]{:S(2)}, u32[]{:S(2)}) %collective-permute-start.8) | collective-permute-done | bytes 3145760 | tf_op jit(solution)/shard_map/ppermute | solution.py:19
  280.1 27.0 %fusion.47 = f32[1,32,2,192,128]{4,3,2,1,0:T(8,128)S(1)} fusion(f32[32,2,192,128]{3,2,1,0:T(8,128)} %get-tuple-element.6, f32[32,2,192,128]{3,2,1,0:T(8,128)} %get-tuple-element.4, f32[32,2,192,128]{3,2,1,0:T(8,128)} %copy-done, f32[32,1,192,128]{3,2,1,0:T(8,128)} %collective-permute-done.9, f32[32,1,192,128]{3,2,1,0:T(8,128)} %collective-permute-done.8, ...), kind=kLoop, calls=%fused_computation.65 | loop fusion | flops 48758784 | bytes 32636952 | tf_op jit(solution)/shard_map/stack | solution.py:81
  310.3 7.6 %copy.32 = f32[2,16,2,192,128]{4,2,1,0,3:T(2,128)} copy(f32[2,16,2,192,128]{4,3,2,1,0:T(8,128)S(1)} %get-tuple-element.10) | data formatting | bytes 12582912 | tf_op jit(solution)/shard_map/slice | solution.py:96
  317.9 5.3 all-to-all-start
  323.1 10.2 %copy.34 = f32[2,16,2,192,128]{4,2,1,0,3:T(2,128)} copy(f32[2,16,2,192,128]{4,3,2,1,0:T(8,128)} %get-tuple-element.9) | data formatting | bytes 12582912 | tf_op jit(solution)/shard_map/slice | solution.py:97
  333.4 51.1 %all-to-all-done = f32[2,16,2,192,128]{4,2,1,0,3:T(2,128)} async-done(((f32[2,16,2,192,128]{4,2,1,0,3:T(2,128)}), f32[2,16,2,192,128]{4,2,1,0,3:T(2,128)}, u32[]{:S(2)}, u32[]{:S(2)}) %all-to-all-start) | async-done | bytes 6291488 | tf_op jit(solution)/shard_map/all_to_all | solution.py:99
  384.5 5.2 all-to-all-start.1
  390.0 9.0 %copy.41 = f32[2,16,2,4,48,128]{5,4,2,1,3,0:T(8,128)} copy(f32[2,16,2,4,48,128]{5,2,1,0,4,3:T(2,128)} %bitcast.12) | data formatting | bytes 12582912 | tf_op jit(solution)/shard_map/all_to_all | solution.py:99
  399.0 7.5 %reshape.20 = f32[128,12288]{1,0:T(8,128)} reshape(f32[2,4,16,2,48,128]{5,4,3,2,1,0:T(8,128)} %bitcast.32) | data formatting | bytes 12582912 | tf_op jit(solution)/shard_map/reshape | solution.py:103
  406.5 25.3 %all-to-all-done.1 = f32[2,16,2,192,128]{4,2,1,0,3:T(2,128)} async-done(((f32[2,16,2,192,128]{4,2,1,0,3:T(2,128)}), f32[2,16,2,192,128]{4,2,1,0,3:T(2,128)}, u32[]{:S(2)}, u32[]{:S(2)}) %all-to-all-start.1) | async-done | bytes 6291488 | tf_op jit(solution)/shard_map/all_to_all | solution.py:100
  431.7 9.0 %copy.40 = f32[2,16,2,4,48,128]{5,4,2,1,3,0:T(8,128)} copy(f32[2,16,2,4,48,128]{5,2,1,0,4,3:T(2,128)} %bitcast.15) | data formatting | bytes 12582912 | tf_op jit(solution)/shard_map/all_to_all | solution.py:100
  440.8 7.4 %reshape.21 = f32[128,12288]{1,0:T(8,128)} reshape(f32[2,4,16,2,48,128]{5,4,3,2,1,0:T(8,128)} %bitcast.34) | data formatting | bytes 12582912 | tf_op jit(solution)/shard_map/reshape | solution.py:104
  448.2 8.8 %fusion.109 = f32[128,128]{1,0:T(8,128)} fusion(f32[128,12288]{1,0:T(8,128)} %reshape.20, f32[128,12288]{1,0:T(8,128)} %reshape.21), kind=kOutput, calls=%fused_computation.151 | convolution fusion | flops 2415919104 | bytes 12648448 | tf_op jit(solution)/shard_map/dot_general | solution.py:105
  457.1 178.4 %all-reduce.12.cloned.1.call-done = f32[128,128]{1,0:T(8,128)} async-done(((f32[128,128]{1,0:T(8,128)}), f32[128,128]{1,0:T(8,128)}) %all-reduce.12.cloned.1.call-update) | async-done | bytes 65552 | tf_op jit(solution)/shard_map/psum | solution.py:114
  (38 shorter events, 30.5 us)
Async XLA Ops:
  7.2 8.6 %copy-start.5 = (f32[16,2,192,128]{3,2,1,0:T(8,128)S(1)}, f32[16,2,192,128]{3,2,1,0:T(8,128)}, u32[]{:S(2)}) copy-start(f32[16,2,192,128]{3,2,1,0:T(8,128)} %param.6) | copy-start | bytes 9437188
  20.9 4.6 copy-start.1
  20.9 11.4 %copy-start.7 = (f32[8]{0:T(128)S(1)}, f32[8]{0:T(128)}, u32[]{:S(2)}) copy-start(f32[8]{0:T(128)} %param.8) | copy-start | bytes 100
  20.9 12.1 %copy-start.6 = (s32[2,192,128]{2,1,0:T(8,128)S(1)}, s32[2,192,128]{2,1,0:T(8,128)}, u32[]{:S(2)}) copy-start(s32[2,192,128]{2,1,0:T(8,128)} %param.7) | copy-start | bytes 589828
  25.4 42.5 %collective-permute-start.1 = (f32[32,1,192,128]{3,2,1,0:T(8,128)}, f32[32,1,192,128]{3,2,1,0:T(8,128)}, u32[]{:S(2)}, u32[]{:S(2)}) collective-permute-start(f32[32,1,192,128]{3,2,1,0:T(8,128)} %get-tuple-element.22), channel_id=1, source_target_pairs={{4,0},{8,4},{12,8},{16,12},{20,16},{24,20},{28,24},{32,28},{36,32}... | collective-permute-start | bytes 9437192 | tf_op jit(solution)/shard_map/ppermute | solution.py:19
  28.8 39.2 %collective-permute-start.3 = (f32[32,1,192,128]{3,2,1,0:T(8,128)}, f32[32,1,192,128]{3,2,1,0:T(8,128)}, u32[]{:S(2)}, u32[]{:S(2)}) collective-permute-start(f32[32,1,192,128]{3,2,1,0:T(8,128)} %get-tuple-element.23), channel_id=1, source_target_pairs={{0,4},{4,8},{8,12},{12,16},{16,20},{20,24},{24,28},{28,32},{32,36}... | collective-permute-start | bytes 9437192 | tf_op jit(solution)/shard_map/ppermute | solution.py:16
  38.2 28.4 %collective-permute-start = (f32[1,192,128]{2,1,0:T(8,128)S(1)}, f32[1,192,128]{2,1,0:T(8,128)S(1)}, u32[]{:S(2)}, u32[]{:S(2)}) collective-permute-start(f32[1,192,128]{2,1,0:T(8,128)S(1)} %get-tuple-element.30), channel_id=1, source_target_pairs={{4,0},{8,4},{12,8},{16,12},{20,16},{24,20},{28,24},{32,28},{36,32}... | collective-permute-start | bytes 294920 | tf_op jit(solution)/shard_map/ppermute | solution.py:19
  40.7 27.1 %collective-permute-start.2 = (f32[1,192,128]{2,1,0:T(8,128)S(1)}, f32[1,192,128]{2,1,0:T(8,128)S(1)}, u32[]{:S(2)}, u32[]{:S(2)}) collective-permute-start(f32[1,192,128]{2,1,0:T(8,128)S(1)} %get-tuple-element.31), channel_id=1, source_target_pairs={{0,4},{4,8},{8,12},{12,16},{16,20},{20,24},{24,28},{28,32},{32,36}... | collective-permute-start | bytes 294920 | tf_op jit(solution)/shard_map/ppermute | solution.py:16
  91.3 4.6 copy-start.3
  95.9 39.6 %collective-permute-start.4 = (f32[32,1,192,128]{3,2,1,0:T(8,128)}, f32[32,1,192,128]{3,2,1,0:T(8,128)}, u32[]{:S(2)}, u32[]{:S(2)}) collective-permute-start(f32[32,1,192,128]{3,2,1,0:T(8,128)} %get-tuple-element.20), channel_id=1, source_target_pairs={{4,0},{8,4},{12,8},{16,12},{20,16},{24,20},{28,24},{32,28},{36,32}... | collective-permute-start | bytes 9437192 | tf_op jit(solution)/shard_map/ppermute | solution.py:19
  97.8 38.9 %collective-permute-start.5 = (f32[32,1,192,128]{3,2,1,0:T(8,128)}, f32[32,1,192,128]{3,2,1,0:T(8,128)}, u32[]{:S(2)}, u32[]{:S(2)}) collective-permute-start(f32[32,1,192,128]{3,2,1,0:T(8,128)} %get-tuple-element.21), channel_id=1, source_target_pairs={{0,4},{4,8},{8,12},{12,16},{16,20},{20,24},{24,28},{28,32},{32,36}... | collective-permute-start | bytes 9437192 | tf_op jit(solution)/shard_map/ppermute | solution.py:16
  162.7 4.6 copy-start.2
  167.3 39.6 %collective-permute-start.6 = (f32[32,1,192,128]{3,2,1,0:T(8,128)}, f32[32,1,192,128]{3,2,1,0:T(8,128)}, u32[]{:S(2)}, u32[]{:S(2)}) collective-permute-start(f32[32,1,192,128]{3,2,1,0:T(8,128)} %get-tuple-element.18), channel_id=1, source_target_pairs={{4,0},{8,4},{12,8},{16,12},{20,16},{24,20},{28,24},{32,28},{36,32}... | collective-permute-start | bytes 9437192 | tf_op jit(solution)/shard_map/ppermute | solution.py:19
  169.2 38.9 %collective-permute-start.7 = (f32[32,1,192,128]{3,2,1,0:T(8,128)}, f32[32,1,192,128]{3,2,1,0:T(8,128)}, u32[]{:S(2)}, u32[]{:S(2)}) collective-permute-start(f32[32,1,192,128]{3,2,1,0:T(8,128)} %get-tuple-element.19), channel_id=1, source_target_pairs={{0,4},{4,8},{8,12},{12,16},{16,20},{20,24},{24,28},{28,32},{32,36}... | collective-permute-start | bytes 9437192 | tf_op jit(solution)/shard_map/ppermute | solution.py:16
  234.7 4.6 copy-start
  239.3 39.6 %collective-permute-start.8 = (f32[32,1,192,128]{3,2,1,0:T(8,128)}, f32[32,1,192,128]{3,2,1,0:T(8,128)}, u32[]{:S(2)}, u32[]{:S(2)}) collective-permute-start(f32[32,1,192,128]{3,2,1,0:T(8,128)} %get-tuple-element.15), channel_id=1, source_target_pairs={{4,0},{8,4},{12,8},{16,12},{20,16},{24,20},{28,24},{32,28},{36,32}... | collective-permute-start | bytes 9437192 | tf_op jit(solution)/shard_map/ppermute | solution.py:19
  241.2 38.9 %collective-permute-start.9 = (f32[32,1,192,128]{3,2,1,0:T(8,128)}, f32[32,1,192,128]{3,2,1,0:T(8,128)}, u32[]{:S(2)}, u32[]{:S(2)}) collective-permute-start(f32[32,1,192,128]{3,2,1,0:T(8,128)} %get-tuple-element.16), channel_id=1, source_target_pairs={{0,4},{4,8},{8,12},{12,16},{16,20},{20,24},{24,28},{28,32},{32,36}... | collective-permute-start | bytes 9437192 | tf_op jit(solution)/shard_map/ppermute | solution.py:16
  280.1 27.0 %copy-start.4 = (f32[1,32,2,192,128]{4,3,2,1,0:T(8,128)S(1)}, f32[1,32,2,192,128]{4,3,2,1,0:T(8,128)}, u32[]{:S(2)}) copy-start(f32[1,32,2,192,128]{4,3,2,1,0:T(8,128)} %get-tuple-element.17) | copy-start | bytes 18874372
  317.9 66.6 %all-to-all-start = ((f32[2,16,2,192,128]{4,2,1,0,3:T(2,128)}), f32[2,16,2,192,128]{4,2,1,0,3:T(2,128)}, u32[]{:S(2)}, u32[]{:S(2)}) async-start(f32[2,16,2,192,128]{4,2,1,0,3:T(2,128)} %copy.32), calls=%async_computation | async-start | bytes 12582912 | tf_op jit(solution)/shard_map/all_to_all | solution.py:99
  384.5 47.3 %all-to-all-start.1 = ((f32[2,16,2,192,128]{4,2,1,0,3:T(2,128)}), f32[2,16,2,192,128]{4,2,1,0,3:T(2,128)}, u32[]{:S(2)}, u32[]{:S(2)}) async-start(f32[2,16,2,192,128]{4,2,1,0,3:T(2,128)} %copy.34), calls=%async_computation.1 | async-start | bytes 12582912 | tf_op jit(solution)/shard_map/all_to_all | solution.py:100
  389.7 245.7 %all-reduce.12.cloned.1.call-start = ((), (), s32[]{:S(2)}) async-start(), calls=%async_computation.2 | async-start | bytes 131072 | tf_op jit(solution)/shard_map/psum | solution.py:114
Sparse Core Ops, SparseCore 0:
  457.2 178.1 all-reduce.11
where the time goes:
time: 645 us; the launch traced here: 644 us
  waiting for transfers between devices  376 us (58%)
  other arithmetic  118 us (18%)
  local copies, waits for them, and re-layouts  76.2 us (12%)
  starting transfers between devices  42.3 us (7%)
  between operations  21.9 us (3%)
  matrix products  8.8 us (1%)
    psum x1, waiting for transfers between devices, body(): whole_sum = lax.psum(partial_value, ('slab', 'col'))  178 us
    ppermute x5, waiting for transfers between devices, extended(): lax.ppermute(lax.slice_in_dim(block, 0, width, axis=dim), axis, backward)  117 us
    all_to_all x1, waiting for transfers between devices, body(): lax.all_to_all(ctrl_local, 'col', split_axis=3, concat_axis=1, tiled=True)  51.1 us
    add x2, other arithmetic, solve_slabs(): rho_next * rho_now * direction + 2.0 * rho_next / half_span * residual  49.9 us
    another operation x2, other arithmetic, run_segments(): return jnp.stack(factors)  30.2 us
    div x2, other arithmetic, solve_slabs(): direction = right_side / mid_eig  29.2 us
    all_to_all x1, waiting for transfers between devices, body(): lax.all_to_all(obsv_local, 'col', split_axis=3, concat_axis=1, tiled=True)  25.3 us
    ppermute x5, starting transfers between devices, extended(): lax.ppermute(lax.slice_in_dim(block, block.shape[dim] - width, None, axis...  19.9 us
  transfers between devices with their start and end apart: 13, of which 11 were waited for; matrix products, arithmetic and copies ran while one was open for 5% of the time, Pallas kernels for 0%

commit v1 on v0

--- a/solution.py
+++ b/solution.py
@@ -6,6 +6,22 @@
 
 ADI = 2
 STEPS = 3
+
+
+def exchange_in_pairs(array, axis, split, join):
+    ways, here = (lax.axis_size(axis), lax.axis_index(axis))
+    width = array.shape[split] // ways
+    dims = list(array.shape)
+    dims[split] = width
+    height = dims[join]
+    dims[join] = height * ways
+    full = jnp.zeros(dims, array.dtype)
+    for mask in range(ways):
+        part = lax.dynamic_slice_in_dim(array, (here ^ mask) * width, width, axis=split)
+        if mask:
+            part = lax.ppermute(part, axis, [(d, d ^ mask) for d in range(ways)])
+        full = lax.dynamic_update_slice_in_dim(full, part, (here ^ mask) * height, axis=join)
+    return full
 
 
 def extended(block, sides, width):
@@ -97,7 +113,7 @@
     obsv_local = factor_stack[:, col_local:]
     ctrl_cols, obsv_cols = (
         lax.all_to_all(ctrl_local, "col", split_axis=3, concat_axis=1, tiled=True),
-        lax.all_to_all(obsv_local, "col", split_axis=3, concat_axis=1, tiled=True),
+        exchange_in_pairs(obsv_local, "col", 3, 1),
     )
     row_count = ctrl_cols.shape[0] * ctrl_cols.shape[1]
     ctrl_flat = ctrl_cols.reshape(row_count, -1)

time: 645 us -> 651 us (level)
  waiting for transfers between devices: 376 us -> 389 us
    ppermute x0 -> x3, waiting for transfers between devices: none -> 92.9 us  [exchange_in_pairs(): part = lax.ppermute(part, axis, [(d, d ^ mask) for d in range(ways)])]
    all_to_all x1, waiting for transfers between devices: 51.1 us -> 0.01 us  [body(): lax.all_to_all(ctrl_local, 'col', split_axis=3, concat_axis=1, tiled=True)]
    all_to_all x1 -> x0, waiting for transfers between devices: 25.3 us -> none  [body(): lax.all_to_all(obsv_local, 'col', split_axis=3, concat_axis=1, tiled=True)]
    slice x2 -> x0, local copies, waits for them, and re-layouts: 17.8 us -> none  [the longest x1 10.2 us: body(): obsv_local = factor_stack[:, col_local:]]
    unnamed x17 -> x26, local copies, waits for them, and re-layouts: 8.16 us -> 22 us
    all_to_all x1 -> x0, local copies, waits for them, and re-layouts: 9.04 us -> none  [body(): lax.all_to_all(obsv_local, 'col', split_axis=3, concat_axis=1, tiled=True)]
    dynamic_update_slice x0 -> x3, local copies, waits for them, and re-layouts: none -> 7.97 us  [exchange_in_pairs(): lax.dynamic_update_slice_in_dim(full, part, (here ^ mask) * height, axis=...]
    another operation x2 -> x3, other arithmetic: 30.2 us -> 31 us  [run_segments(): return jnp.stack(factors)]
  transfers between devices with their start and end apart: 13 -> 15, of which waited for: 11 -> 11; matrix products, arithmetic and copies ran while one was open for 5% -> 4% of each run, Pallas kernels for 0% -> 0%
where the time goes in v1:
time: 651 us; the launch traced here: 650 us
  waiting for transfers between devices  389 us (60%)
  other arithmetic  119 us (18%)
  local copies, waits for them, and re-layouts  71.5 us (11%)
  starting transfers between devices  40.6 us (6%)
  between operations  21.6 us (3%)
  matrix products  8.81 us (1%)
    psum x1, waiting for transfers between devices, body(): whole_sum = lax.psum(partial_value, ('slab', 'col'))  174 us
    ppermute x5, waiting for transfers between devices, extended(): lax.ppermute(lax.slice_in_dim(block, 0, width, axis=dim), axis, backward)  117 us
    ppermute x3, waiting for transfers between devices, exchange_in_pairs(): part = lax.ppermute(part, axis, [(d, d ^ mask) for d in range(ways)])  92.9 us
    add x2, other arithmetic, solve_slabs(): rho_next * rho_now * direction + 2.0 * rho_next / half_span * residual  49.8 us
    another operation x3, other arithmetic, run_segments(): return jnp.stack(factors)  31 us
    div x2, other arithmetic, solve_slabs(): direction = right_side / mid_eig  29.1 us
    unnamed x26, local copies, waits for them, and re-layouts  22 us
    ppermute x5, starting transfers between devices, extended(): lax.ppermute(lax.slice_in_dim(block, block.shape[dim] - width, None, axis...  19.9 us
  transfers between devices with their start and end apart: 15, of which 11 were waited for; matrix products, arithmetic and copies ran while one was open for 4% of the time, Pallas kernels for 0%

profile of v1, /device:TPU:1, one launch (start us, length us, event | category | flops | bytes accessed | tf_op | source)
XLA Modules:
  0.0 649.9 jit_solution(6869410976651268178)
XLA Ops:
  11.8 3.9 constant_dynamic-update-slice_fusion.1
  17.6 3.2 broadcast_divide_fusion.1
  20.8 3.3 fusion.110
  25.4 3.3 collective-permute-start.1
  28.7 3.5 collective-permute-start.3
  32.9 5.1 select_add_fusion
  40.5 3.1 collective-permute-start.2
  44.4 22.1 %collective-permute-done = f32[1,192,128]{2,1,0:T(8,128)S(1)} collective-permute-done((f32[1,192,128]{2,1,0:T(8,128)S(1)}, f32[1,192,128]{2,1,0:T(8,128)S(1)}, u32[]{:S(2)}, u32[]{:S(2)}) %collective-permute-start) | collective-permute-done | bytes 98336 | tf_op jit(solution)/shard_map/ppermute | solution.py:35
  67.9 23.3 %multiply_add_fusion.1 = (f32[32,2,192,128]{3,2,1,0:T(8,128)S(1)}, f32[32,2,192,128]{3,2,1,0:T(8,128)}) fusion(f32[32,2,192,128]{3,2,1,0:T(8,128)} %copy-done.3, f32[]{:T(128)S(6)} %div.53, f32[]{:T(128)S(6)} %mul.378, f32[32,2,192,128]{3,2,1,0:T(8,128)} %constant_dynamic-update-slice_fusion, f32[]{:T(128)} %bitcast, ...), kind=kLoop, calls=%fused_computation.115 | loop fusion | flops 39321600 | bytes 32636940 | tf_op jit(solution)/shard_map/add | solution.py:82
  91.2 3.3 fusion.109
  97.8 4.4 collective-permute-start.5
  103.4 32.1 %collective-permute-done.4 = f32[32,1,192,128]{3,2,1,0:T(8,128)} collective-permute-done((f32[32,1,192,128]{3,2,1,0:T(8,128)}, f32[32,1,192,128]{3,2,1,0:T(8,128)}, u32[]{:S(2)}, u32[]{:S(2)}) %collective-permute-start.4) | collective-permute-done | bytes 3145760 | tf_op jit(solution)/shard_map/ppermute | solution.py:35
  136.7 25.9 %broadcast_divide_fusion = (f32[32,2,192,128]{3,2,1,0:T(8,128)S(1)}, f32[32,2,192,128]{3,2,1,0:T(8,128)}) fusion(f32[]{:T(128)S(6)} %mul.421, f32[32,2,192,128]{3,2,1,0:T(8,128)} %get-tuple-element.8, f32[32,2,192,128]{3,2,1,0:T(8,128)} %copy-done.5, f32[]{:T(128)} %bitcast, f32[2,192,128]{2,1,0:T(8,128)S(1)} %get-tuple-element.29, ...), kind=kLoop, calls=%fused_computation.124 | loop fusion | flops 45613056 | bytes 38928404 | tf_op jit(solution)/shard_map/div | solution.py:75
  162.5 3.8 fusion.108
  169.1 4.4 collective-permute-start.7
  174.9 31.9 %collective-permute-done.6 = f32[32,1,192,128]{3,2,1,0:T(8,128)} collective-permute-done((f32[32,1,192,128]{3,2,1,0:T(8,128)}, f32[32,1,192,128]{3,2,1,0:T(8,128)}, u32[]{:S(2)}, u32[]{:S(2)}) %collective-permute-start.6) | collective-permute-done | bytes 3145760 | tf_op jit(solution)/shard_map/ppermute | solution.py:35
  208.0 26.5 %multiply_add_fusion = (f32[32,2,192,128]{3,2,1,0:T(8,128)S(1)}, f32[32,2,192,128]{3,2,1,0:T(8,128)}, f32[1,32,2,192,128]{4,3,2,1,0:T(8,128)}) fusion(f32[]{:T(128)S(6)} %div.61, f32[]{:T(128)S(6)} %mul.424, f32[32,2,192,128]{3,2,1,0:T(8,128)} %get-tuple-element.6, f32[]{:T(128)S(6)} %mul.421, f32[32,2,192,128]{3,2,1,0:T(8,128)} %copy-done.4, f32[]{:T(128)} %bitcast.10, ...), kind=kLoop, calls=%fused_computation.113 | loop fusion | flops 42467328 | bytes 38928404 | tf_op jit(solution)/shard_map/add | solution.py:82
  234.5 3.4 fusion.107
  241.1 4.6 collective-permute-start.9
  247.6 31.3 %collective-permute-done.8 = f32[32,1,192,128]{3,2,1,0:T(8,128)} collective-permute-done((f32[32,1,192,128]{3,2,1,0:T(8,128)}, f32[32,1,192,128]{3,2,1,0:T(8,128)}, u32[]{:S(2)}, u32[]{:S(2)}) %collective-permute-start.8) | collective-permute-done | bytes 3145760 | tf_op jit(solution)/shard_map/ppermute | solution.py:35
  280.0 26.9 %fusion.47 = f32[1,32,2,192,128]{4,3,2,1,0:T(8,128)S(1)} fusion(f32[32,2,192,128]{3,2,1,0:T(8,128)} %get-tuple-element.6, f32[32,2,192,128]{3,2,1,0:T(8,128)} %get-tuple-element.4, f32[32,2,192,128]{3,2,1,0:T(8,128)} %copy-done.2, f32[32,1,192,128]{3,2,1,0:T(8,128)} %collective-permute-done.9, f32[32,1,192,128]{3,2,1,0:T(8,128)} %collective-permute-done.8, ...), kind=kLoop, calls=%fused_computation.65 | loop fusion | flops 48758784 | bytes 32636952 | tf_op jit(solution)/shard_map/stack | solution.py:97
  309.7 6.3 copy.26
  316.0 5.3 all-to-all-start
  324.1 3.7 fusion.87
  327.8 2.7 copy-done.6
  334.4 77.2 %collective-permute-done.10 = f32[2,16,2,48,128]{4,3,2,1,0:T(8,128)} collective-permute-done((f32[2,16,2,48,128]{4,3,2,1,0:T(8,128)}, f32[2,16,2,48,128]{4,3,2,1,0:T(8,128)}, u32[]{:S(2)}, u32[]{:S(2)}) %collective-permute-start.10) | collective-permute-done | bytes 1572896 | tf_op jit(solution)/shard_map/ppermute | solution.py:22
  414.3 15.7 %collective-permute-done.11 = f32[2,16,2,48,128]{4,3,2,1,0:T(8,128)} collective-permute-done((f32[2,16,2,48,128]{4,3,2,1,0:T(8,128)S(1)}, f32[2,16,2,48,128]{4,3,2,1,0:T(8,128)}, u32[]{:S(2)}, u32[]{:S(2)}) %collective-permute-start.11) | collective-permute-done | bytes 1572896 | tf_op jit(solution)/shard_map/ppermute | solution.py:22
  435.3 7.5 %reshape.20 = f32[128,12288]{1,0:T(8,128)} reshape(f32[2,64,2,48,128]{4,3,2,1,0:T(8,128)} %constant_dynamic-update-slice_fusion.2) | data formatting | bytes 12582912 | tf_op jit(solution)/shard_map/reshape | solution.py:120
  442.8 9.0 %copy.29 = f32[2,16,2,4,48,128]{5,4,2,1,3,0:T(8,128)} copy(f32[2,16,2,4,48,128]{5,1,2,0,4,3:T(8,128)} %bitcast.12) | data formatting | bytes 12582912 | tf_op jit(solution)/shard_map/all_to_all | solution.py:115
  451.8 7.4 %reshape.19 = f32[128,12288]{1,0:T(8,128)} reshape(f32[2,4,16,2,48,128]{5,4,3,2,1,0:T(8,128)} %bitcast.28) | data formatting | bytes 12582912 | tf_op jit(solution)/shard_map/reshape | solution.py:119
  459.2 8.8 %fusion.114 = f32[128,128]{1,0:T(8,128)} fusion(f32[128,12288]{1,0:T(8,128)} %reshape.19, f32[128,12288]{1,0:T(8,128)} %reshape.20), kind=kOutput, calls=%fused_computation.165 | convolution fusion | flops 2415919104 | bytes 12648448 | tf_op jit(solution)/shard_map/dot_general | solution.py:121
  468.1 173.6 %all-reduce.12.cloned.1.call-done = f32[128,128]{1,0:T(8,128)} async-done(((f32[128,128]{1,0:T(8,128)}), f32[128,128]{1,0:T(8,128)}) %all-reduce.12.cloned.1.call-update) | async-done | bytes 65552 | tf_op jit(solution)/shard_map/psum | solution.py:130
  (54 shorter events, 41.8 us)
Async XLA Ops:
  7.2 8.5 %copy-start.7 = (f32[16,2,192,128]{3,2,1,0:T(8,128)S(1)}, f32[16,2,192,128]{3,2,1,0:T(8,128)}, u32[]{:S(2)}) copy-start(f32[16,2,192,128]{3,2,1,0:T(8,128)} %param.6) | copy-start | bytes 9437188
  20.8 4.6 copy-start.3
  20.8 11.4 %copy-start.9 = (f32[8]{0:T(128)S(1)}, f32[8]{0:T(128)}, u32[]{:S(2)}) copy-start(f32[8]{0:T(128)} %param.8) | copy-start | bytes 100
  20.8 12.1 %copy-start.8 = (s32[2,192,128]{2,1,0:T(8,128)S(1)}, s32[2,192,128]{2,1,0:T(8,128)}, u32[]{:S(2)}) copy-start(s32[2,192,128]{2,1,0:T(8,128)} %param.7) | copy-start | bytes 589828
  25.4 42.5 %collective-permute-start.1 = (f32[32,1,192,128]{3,2,1,0:T(8,128)}, f32[32,1,192,128]{3,2,1,0:T(8,128)}, u32[]{:S(2)}, u32[]{:S(2)}) collective-permute-start(f32[32,1,192,128]{3,2,1,0:T(8,128)} %get-tuple-element.22), channel_id=1, source_target_pairs={{4,0},{8,4},{12,8},{16,12},{20,16},{24,20},{28,24},{32,28},{36,32}... | collective-permute-start | bytes 9437192 | tf_op jit(solution)/shard_map/ppermute | solution.py:35
  28.7 39.2 %collective-permute-start.3 = (f32[32,1,192,128]{3,2,1,0:T(8,128)}, f32[32,1,192,128]{3,2,1,0:T(8,128)}, u32[]{:S(2)}, u32[]{:S(2)}) collective-permute-start(f32[32,1,192,128]{3,2,1,0:T(8,128)} %get-tuple-element.23), channel_id=1, source_target_pairs={{0,4},{4,8},{8,12},{12,16},{16,20},{20,24},{24,28},{28,32},{32,36}... | collective-permute-start | bytes 9437192 | tf_op jit(solution)/shard_map/ppermute | solution.py:32
  38.0 28.5 %collective-permute-start = (f32[1,192,128]{2,1,0:T(8,128)S(1)}, f32[1,192,128]{2,1,0:T(8,128)S(1)}, u32[]{:S(2)}, u32[]{:S(2)}) collective-permute-start(f32[1,192,128]{2,1,0:T(8,128)S(1)} %get-tuple-element.30), channel_id=1, source_target_pairs={{4,0},{8,4},{12,8},{16,12},{20,16},{24,20},{28,24},{32,28},{36,32}... | collective-permute-start | bytes 294920 | tf_op jit(solution)/shard_map/ppermute | solution.py:35
  40.5 27.2 %collective-permute-start.2 = (f32[1,192,128]{2,1,0:T(8,128)S(1)}, f32[1,192,128]{2,1,0:T(8,128)S(1)}, u32[]{:S(2)}, u32[]{:S(2)}) collective-permute-start(f32[1,192,128]{2,1,0:T(8,128)S(1)} %get-tuple-element.31), channel_id=1, source_target_pairs={{0,4},{4,8},{8,12},{12,16},{16,20},{20,24},{24,28},{28,32},{32,36}... | collective-permute-start | bytes 294920 | tf_op jit(solution)/shard_map/ppermute | solution.py:32
  91.2 4.6 copy-start.5
  95.8 39.6 %collective-permute-start.4 = (f32[32,1,192,128]{3,2,1,0:T(8,128)}, f32[32,1,192,128]{3,2,1,0:T(8,128)}, u32[]{:S(2)}, u32[]{:S(2)}) collective-permute-start(f32[32,1,192,128]{3,2,1,0:T(8,128)} %get-tuple-element.20), channel_id=1, source_target_pairs={{4,0},{8,4},{12,8},{16,12},{20,16},{24,20},{28,24},{32,28},{36,32}... | collective-permute-start | bytes 9437192 | tf_op jit(solution)/shard_map/ppermute | solution.py:35
  97.8 38.9 %collective-permute-start.5 = (f32[32,1,192,128]{3,2,1,0:T(8,128)}, f32[32,1,192,128]{3,2,1,0:T(8,128)}, u32[]{:S(2)}, u32[]{:S(2)}) collective-permute-start(f32[32,1,192,128]{3,2,1,0:T(8,128)} %get-tuple-element.21), channel_id=1, source_target_pairs={{0,4},{4,8},{8,12},{12,16},{16,20},{20,24},{24,28},{28,32},{32,36}... | collective-permute-start | bytes 9437192 | tf_op jit(solution)/shard_map/ppermute | solution.py:32
  162.5 4.6 copy-start.4
  167.1 39.6 %collective-permute-start.6 = (f32[32,1,192,128]{3,2,1,0:T(8,128)}, f32[32,1,192,128]{3,2,1,0:T(8,128)}, u32[]{:S(2)}, u32[]{:S(2)}) collective-permute-start(f32[32,1,192,128]{3,2,1,0:T(8,128)} %get-tuple-element.18), channel_id=1, source_target_pairs={{4,0},{8,4},{12,8},{16,12},{20,16},{24,20},{28,24},{32,28},{36,32}... | collective-permute-start | bytes 9437192 | tf_op jit(solution)/shard_map/ppermute | solution.py:35
  169.1 38.9 %collective-permute-start.7 = (f32[32,1,192,128]{3,2,1,0:T(8,128)}, f32[32,1,192,128]{3,2,1,0:T(8,128)}, u32[]{:S(2)}, u32[]{:S(2)}) collective-permute-start(f32[32,1,192,128]{3,2,1,0:T(8,128)} %get-tuple-element.19), channel_id=1, source_target_pairs={{0,4},{4,8},{8,12},{12,16},{16,20},{20,24},{24,28},{28,32},{32,36}... | collective-permute-start | bytes 9437192 | tf_op jit(solution)/shard_map/ppermute | solution.py:32
  234.5 4.7 copy-start.2
  234.5 72.5 %slice-start = ((s8[6291456]{0:T(1024)(128)(4,1)}), s8[2097152]{0:T(1024)(128)(4,1)S(1)}, s32[]{:S(2)}) async-start(s8[6291456]{0:T(1024)(128)(4,1)} %bitcast.26), calls=%async_computation.2 | async-start | bytes 4194304
  239.2 39.6 %collective-permute-start.8 = (f32[32,1,192,128]{3,2,1,0:T(8,128)}, f32[32,1,192,128]{3,2,1,0:T(8,128)}, u32[]{:S(2)}, u32[]{:S(2)}) collective-permute-start(f32[32,1,192,128]{3,2,1,0:T(8,128)} %get-tuple-element.15), channel_id=1, source_target_pairs={{4,0},{8,4},{12,8},{16,12},{20,16},{24,20},{28,24},{32,28},{36,32}... | collective-permute-start | bytes 9437192 | tf_op jit(solution)/shard_map/ppermute | solution.py:35
  241.1 38.9 %collective-permute-start.9 = (f32[32,1,192,128]{3,2,1,0:T(8,128)}, f32[32,1,192,128]{3,2,1,0:T(8,128)}, u32[]{:S(2)}, u32[]{:S(2)}) collective-permute-start(f32[32,1,192,128]{3,2,1,0:T(8,128)} %get-tuple-element.16), channel_id=1, source_target_pairs={{0,4},{4,8},{8,12},{12,16},{16,20},{20,24},{24,28},{28,32},{32,36}... | collective-permute-start | bytes 9437192 | tf_op jit(solution)/shard_map/ppermute | solution.py:32
  280.0 27.0 %slice-start.1 = ((s8[6291456]{0:T(1024)(128)(4,1)}), s8[4194304]{0:T(1024)(128)(4,1)S(1)}, s32[]{:S(2)}) async-start(s8[6291456]{0:T(1024)(128)(4,1)} %bitcast.26), calls=%async_computation.3 | async-start | bytes 8388608
  307.0 2.7 copy-start
  316.0 126.7 %all-to-all-start = ((f32[2,16,2,192,128]{4,1,2,0,3:T(8,128)}), f32[2,16,2,192,128]{4,1,2,0,3:T(8,128)}, u32[]{:S(2)}, u32[]{:S(2)}) async-start(f32[2,16,2,192,128]{4,1,2,0,3:T(8,128)} %copy.26), calls=%async_computation | async-start | bytes 12582912 | tf_op jit(solution)/shard_map/all_to_all | solution.py:115
  321.3 320.4 %all-reduce.12.cloned.1.call-start = ((), (), s32[]{:S(2)}) async-start(), calls=%async_computation.1 | async-start | bytes 131072 | tf_op jit(solution)/shard_map/psum | solution.py:130
  321.4 2.8 copy-start.1
  327.8 2.7 copy-start.6
  330.5 81.1 %collective-permute-start.10 = (f32[2,16,2,48,128]{4,3,2,1,0:T(8,128)}, f32[2,16,2,48,128]{4,3,2,1,0:T(8,128)}, u32[]{:S(2)}, u32[]{:S(2)}) collective-permute-start(f32[2,16,2,48,128]{4,3,2,1,0:T(8,128)} %get-tuple-element.11), channel_id=1, source_target_pairs={{0,1},{1,0},{2,3},{3,2},{4,5},{5,4},{6,7},{7,6},{8,9},{9,8},{10,11... | collective-permute-start | bytes 4718600 | tf_op jit(solution)/shard_map/ppermute | solution.py:22
  331.9 98.1 %collective-permute-start.11 = (f32[2,16,2,48,128]{4,3,2,1,0:T(8,128)S(1)}, f32[2,16,2,48,128]{4,3,2,1,0:T(8,128)}, u32[]{:S(2)}, u32[]{:S(2)}) collective-permute-start(f32[2,16,2,48,128]{4,3,2,1,0:T(8,128)S(1)} %get-tuple-element.12), channel_id=1, source_target_pairs={{0,2},{1,3},{2,0},{3,1},{4,6},{5,7},{6,4},{7,5},{8,10},{9,11},{10,... | collective-permute-start | bytes 4718600 | tf_op jit(solution)/shard_map/ppermute | solution.py:22
  334.3 98.4 %collective-permute-start.12 = (f32[2,16,2,48,128]{4,3,2,1,0:T(8,128)S(1)}, f32[2,16,2,48,128]{4,3,2,1,0:T(8,128)}, u32[]{:S(2)}, u32[]{:S(2)}) collective-permute-start(f32[2,16,2,48,128]{4,3,2,1,0:T(8,128)S(1)} %get-tuple-element.9), channel_id=1, source_target_pairs={{0,3},{1,2},{2,1},{3,0},{4,7},{5,6},{6,5},{7,4},{8,11},{9,10},{10,... | collective-permute-start | bytes 4718600 | tf_op jit(solution)/shard_map/ppermute | solution.py:22
Sparse Core Ops, SparseCore 0:
  468.2 173.4 all-reduce.11
